TPU v7x, 512 devices: a whole 4x8x8 slice. The times are simulated.
512 devices in a mesh: src: 16 (over z, y_hi), tgt: 32 (over x, y_lo, core).
Axes of the slice: x: 4, y: 8 (y_hi: 2, y_lo: 4; y = y_hi * 4 + y_lo), z: 8, core: 2. Of those that a mesh axis runs over, the one named last changes fastest.
Arguments:
- coupling: bfloat16 [8192, 16384], P('src', 'tgt'), may hold values from 0.25 to 4
- src_pcs: bfloat16 [50, 8192], P(None, 'src'), may hold values from -24 to 24
- tgt_pcs: bfloat16 [50, 16384], P(None, 'tgt'), may hold values from -24 to 24
- src_mass: float32 [8192], P('src'), may hold values from 0.25 to 4
- tgt_mass: float32 [16384], P('tgt'), may hold values from 0.25 to 4
Outputs:
- log_coupling: float32 [8192, 16384], P('src', 'tgt')
- row_potential: float32 [8192], P('src')
- col_potential: float32 [16384], P('tgt')
All inputs are finite; a program needn't handle non-finite values.
Results may differ from a plain program's by a relative error of at most 0.0019.
Values sent between devices are 32-bit elements; how exact they have to be, the bound alone decides.
A program may use at most 64 MiB of HBM per device.

v0:
```python
import jax
import jax.numpy as jnp
from jax import lax
from jax.sharding import PartitionSpec as P

PCS = 50
ITERS = 4


eps_reg = 0.5
marg_power = 1.0 / (1.0 + eps_reg)
tiny_eps = 1e-06


def row_logmean(shifted, count):
    local_max = jnp.max(shifted, axis=1)
    highest = lax.pmax(local_max, "tgt")
    summed_exp = lax.psum(jnp.sum(jnp.exp(shifted - highest[:, None]), axis=1), "tgt")
    return highest + jnp.log(summed_exp) - jnp.log(jnp.float32(count))


def col_logmean(shifted, count):
    local_max = jnp.max(shifted, axis=0)
    highest = lax.pmax(local_max, "src")
    summed_exp = lax.psum(jnp.sum(jnp.exp(shifted - highest[None, :]), axis=0), "src")
    return highest + jnp.log(summed_exp) - jnp.log(jnp.float32(count))


def shards(coupling, src_pcs, tgt_pcs, src_mass, tgt_mass):
    exact = lax.Precision.HIGHEST
    total_rows = coupling.shape[0] * lax.axis_size("src")
    total_cols = coupling.shape[1] * lax.axis_size("tgt")
    src_float = src_pcs.astype(jnp.float32)
    tgt_float = tgt_pcs.astype(jnp.float32)
    partial_cols = jnp.dot(src_pcs, coupling, preferred_element_type=jnp.float32)
    summed_panel = lax.psum(partial_cols, "src")
    local_moment = jnp.dot(summed_panel, tgt_float.T, precision=exact)
    moment = lax.psum(local_moment, "tgt")
    moment = moment * (total_rows * total_cols) ** (-0.5)
    normed = moment / jnp.sqrt(jnp.mean(moment * moment) + tiny_eps)
    weighted = jnp.dot(normed, tgt_float, precision=exact)
    scores = jnp.dot(src_float.T, weighted, precision=exact) * (2.0 / (eps_reg * PCS))
    log_src = jnp.log(src_mass)
    log_tgt = jnp.log(tgt_mass)
    col_potential = jnp.zeros((coupling.shape[1],), jnp.float32)
    row_potential = jnp.zeros((coupling.shape[0],), jnp.float32)
    for iteration in range(ITERS):
        row_potential = marg_power * (
            log_src - row_logmean(scores + col_potential[None, :], total_cols)
        )
        col_potential = marg_power * (
            log_tgt - col_logmean(scores + row_potential[:, None], total_rows)
        )
    log_coupling = scores + row_potential[:, None] + col_potential[None, :]
    return (log_coupling, row_potential, col_potential)


def solution(mesh):
    in_specs = (P("src", "tgt"), P(None, "src"), P(None, "tgt"), P("src"), P("tgt"))
    out_specs = (P("src", "tgt"), P("src"), P("tgt"))
    return jax.shard_map(shards, mesh=mesh, in_specs=in_specs, out_specs=out_specs, check_vma=False)
```

profile of v0, /device:TPU:1, one launch (start us, length us, event | category | flops | bytes accessed | tf_op | source)
XLA Modules:
  0.0 1285.6 jit_solution(14913943931029631534)
XLA Ops:
  7.2 1.0 copy-done
  8.2 1.7 fusion.7
  9.9 195.1 %all-reduce.2.cloned.1.call-done = f32[50,512]{1,0:T(8,128)} async-done(((f32[50,512]{1,0:T(8,128)}), f32[50,512]{1,0:T(8,128)}) %all-reduce.2.cloned.1.call-update) | async-done | bytes 102416 | tf_op jit(solution)/shard_map/psum | solution.py:36
  205.0 1.1 fusion.8
  206.1 139.2 %psum.71 = f32[50,50]{1,0:T(8,128)S(1)} all-reduce(f32[50,50]{1,0:T(8,128)S(1)} %fusion.8), channel_id=1, replica_groups=mesh['src'=16,'tgt'=32] {'tgt'}, use_global_device_ids=true, to_apply=%region_1.0 | all-reduce | flops 2500 | bytes 20000 | tf_op jit(solution)/shard_map/psum | solution.py:38
  345.4 0.6 multiply_reduce_fusion
  346.9 0.6 copy-done.2
  347.5 0.7 fusion.6
  348.1 72.9 %pmax.56 = f32[512]{0:T(512)S(1)} all-reduce(f32[512]{0:T(512)S(1)} %get-tuple-element.6), channel_id=1, replica_groups=mesh['src'=16,'tgt'=32] {'tgt'}, use_global_device_ids=true, to_apply=%region_4.0 | all-reduce | flops 512 | bytes 4096 | tf_op jit(solution)/shard_map/pmax | solution.py:17
  421.2 67.4 %psum.72 = f32[512]{0:T(512)S(1)} all-reduce(f32[512]{0:T(512)S(1)} %exponential_reduce_fusion.7), channel_id=1, replica_groups=mesh['src'=16,'tgt'=32] {'tgt'}, use_global_device_ids=true, to_apply=%region_6.0 | all-reduce | flops 512 | bytes 4096 | tf_op jit(solution)/shard_map/psum | solution.py:18
  488.8 41.6 %pmax.57 = f32[512]{0:T(512)S(1)} all-reduce(f32[512]{0:T(512)S(1)} %add_reduce_fusion.5), channel_id=1, replica_groups=mesh['src'=16,'tgt'=32] {'src'}, use_global_device_ids=true, to_apply=%region_8.0 | all-reduce | flops 512 | bytes 4096 | tf_op jit(solution)/shard_map/pmax | solution.py:24
  530.4 0.3 exponential_reduce_fusion.6
  530.7 42.7 %psum.73 = f32[512]{0:T(512)S(1)} all-reduce(f32[512]{0:T(512)S(1)} %exponential_reduce_fusion.6), channel_id=1, replica_groups=mesh['src'=16,'tgt'=32] {'src'}, use_global_device_ids=true, to_apply=%region_10.0 | all-reduce | flops 512 | bytes 4096 | tf_op jit(solution)/shard_map/psum | solution.py:25
  573.6 81.8 %pmax.58 = f32[512]{0:T(512)S(1)} all-reduce(f32[512]{0:T(512)S(1)} %add_reduce_fusion.4), channel_id=1, replica_groups=mesh['src'=16,'tgt'=32] {'tgt'}, use_global_device_ids=true, to_apply=%region_12.0 | all-reduce | flops 512 | bytes 4096 | tf_op jit(solution)/shard_map/pmax | solution.py:17
  655.5 0.3 exponential_reduce_fusion.5
  655.7 67.4 %psum.74 = f32[512]{0:T(512)S(1)} all-reduce(f32[512]{0:T(512)S(1)} %exponential_reduce_fusion.5), channel_id=1, replica_groups=mesh['src'=16,'tgt'=32] {'tgt'}, use_global_device_ids=true, to_apply=%region_14.0 | all-reduce | flops 512 | bytes 4096 | tf_op jit(solution)/shard_map/psum | solution.py:18
  723.3 41.6 %pmax.59 = f32[512]{0:T(512)S(1)} all-reduce(f32[512]{0:T(512)S(1)} %add_reduce_fusion.3), channel_id=1, replica_groups=mesh['src'=16,'tgt'=32] {'src'}, use_global_device_ids=true, to_apply=%region_16.0 | all-reduce | flops 512 | bytes 4096 | tf_op jit(solution)/shard_map/pmax | solution.py:24
  764.9 0.3 exponential_reduce_fusion.4
  765.2 42.7 %psum.75 = f32[512]{0:T(512)S(1)} all-reduce(f32[512]{0:T(512)S(1)} %exponential_reduce_fusion.4), channel_id=1, replica_groups=mesh['src'=16,'tgt'=32] {'src'}, use_global_device_ids=true, to_apply=%region_18.0 | all-reduce | flops 512 | bytes 4096 | tf_op jit(solution)/shard_map/psum | solution.py:25
  808.1 81.8 %pmax.60 = f32[512]{0:T(512)S(1)} all-reduce(f32[512]{0:T(512)S(1)} %add_reduce_fusion.2), channel_id=1, replica_groups=mesh['src'=16,'tgt'=32] {'tgt'}, use_global_device_ids=true, to_apply=%region_20.0 | all-reduce | flops 512 | bytes 4096 | tf_op jit(solution)/shard_map/pmax | solution.py:17
  889.9 0.3 exponential_reduce_fusion.3
  890.2 67.4 %psum.76 = f32[512]{0:T(512)S(1)} all-reduce(f32[512]{0:T(512)S(1)} %exponential_reduce_fusion.3), channel_id=1, replica_groups=mesh['src'=16,'tgt'=32] {'tgt'}, use_global_device_ids=true, to_apply=%region_22.0 | all-reduce | flops 512 | bytes 4096 | tf_op jit(solution)/shard_map/psum | solution.py:18
  957.7 41.6 %pmax.61 = f32[512]{0:T(512)S(1)} all-reduce(f32[512]{0:T(512)S(1)} %add_reduce_fusion.1), channel_id=1, replica_groups=mesh['src'=16,'tgt'=32] {'src'}, use_global_device_ids=true, to_apply=%region_24.0 | all-reduce | flops 512 | bytes 4096 | tf_op jit(solution)/shard_map/pmax | solution.py:24
  999.3 0.3 exponential_reduce_fusion.2
  999.7 43.0 %psum.77 = f32[512]{0:T(512)S(1)} all-reduce(f32[512]{0:T(512)S(1)} %exponential_reduce_fusion.2), channel_id=1, replica_groups=mesh['src'=16,'tgt'=32] {'src'}, use_global_device_ids=true, to_apply=%region_26.0 | all-reduce | flops 512 | bytes 4096 | tf_op jit(solution)/shard_map/psum | solution.py:25
  1042.8 81.5 %pmax.62 = f32[512]{0:T(512)S(1)} all-reduce(f32[512]{0:T(512)S(1)} %add_reduce_fusion), channel_id=1, replica_groups=mesh['src'=16,'tgt'=32] {'tgt'}, use_global_device_ids=true, to_apply=%region_28.0 | all-reduce | flops 512 | bytes 4096 | tf_op jit(solution)/shard_map/pmax | solution.py:17
  1124.6 67.4 %psum.78 = f32[512]{0:T(512)S(1)} all-reduce(f32[512]{0:T(512)S(1)} %exponential_reduce_fusion.1), channel_id=1, replica_groups=mesh['src'=16,'tgt'=32] {'tgt'}, use_global_device_ids=true, to_apply=%region_30.0 | all-reduce | flops 512 | bytes 4096 | tf_op jit(solution)/shard_map/psum | solution.py:18
  1192.2 41.6 %pmax.63 = f32[512]{0:T(512)S(1)} all-reduce(f32[512]{0:T(512)S(1)} %add_reduce_fusion.6), channel_id=1, replica_groups=mesh['src'=16,'tgt'=32] {'src'}, use_global_device_ids=true, to_apply=%region_32.0 | all-reduce | flops 512 | bytes 4096 | tf_op jit(solution)/shard_map/pmax | solution.py:24
  1233.8 0.3 exponential_reduce_fusion
  1234.1 42.7 %psum.79 = f32[512]{0:T(512)S(1)} all-reduce(f32[512]{0:T(512)S(1)} %exponential_reduce_fusion), channel_id=1, replica_groups=mesh['src'=16,'tgt'=32] {'src'}, use_global_device_ids=true, to_apply=%region_34.0 | all-reduce | flops 512 | bytes 4096 | tf_op jit(solution)/shard_map/psum | solution.py:25
  1277.0 0.4 copy-done.6
  1277.4 1.3 copy.8
  (32 shorter events, 2.1 us)
Async XLA Ops:
  7.2 1.0 copy-start
  7.2 197.9 %all-reduce.2.cloned.1.call-start = ((), (), s32[]{:S(2)}) async-start(), calls=%async_computation | async-start | bytes 229376 | tf_op jit(solution)/shard_map/psum | solution.py:36
  9.9 195.2 %copy-start.1 = (bf16[50,512]{1,0:T(8,128)(2,1)S(1)}, bf16[50,512]{1,0:T(8,128)(2,1)}, u32[]{:S(2)}) copy-start(bf16[50,512]{1,0:T(8,128)(2,1)} %param.7) | copy-start | bytes 153604
  346.7 0.8 copy-start.2
  421.2 67.4 %copy-start.3 = (f32[512]{0:T(512)S(1)}, f32[512]{0:T(512)}, u32[]{:S(2)}) copy-start(f32[512]{0:T(512)} %param.8) | copy-start | bytes 6148
  530.4 43.0 %copy-start.4 = (f32[512]{0:T(512)S(1)}, f32[512]{0:T(512)}, u32[]{:S(2)}) copy-start(f32[512]{0:T(512)} %param.9) | copy-start | bytes 6148
  1192.0 84.8 %copy-start.5 = (f32[512]{0:T(512)}, f32[512]{0:T(512)S(1)}, u32[]{:S(2)}) copy-start(f32[512]{0:T(512)S(1)} %subtract_multiply_fusion.1) | copy-start | bytes 6148
  1276.9 0.6 copy-start.6
Sparse Core Ops, SparseCore 0:
  11.5 193.5 all-reduce.1
where the time goes:
time: 1300 us; the launch traced here: 1290 us
  blocking collectives  1060 us (82%)
  waiting for transfers between devices  195 us (15%)
  between operations  14.8 us (1%)
    pmax x4, blocking collectives, row_logmean(): highest = lax.pmax(local_max, 'tgt')  318 us
    psum x4, blocking collectives, row_logmean(): lax.psum(jnp.sum(jnp.exp(shifted - highest[:, None]), axis=1), 'tgt')  269 us
    psum x1, waiting for transfers between devices, shards(): summed_panel = lax.psum(partial_cols, 'src')  195 us
    psum x4, blocking collectives, col_logmean(): lax.psum(jnp.sum(jnp.exp(shifted - highest[None, :]), axis=0), 'src')  171 us
    pmax x4, blocking collectives, col_logmean(): highest = lax.pmax(local_max, 'src')  166 us
    psum x1, blocking collectives, shards(): moment = lax.psum(local_moment, 'tgt')  139 us
  transfers between devices with their start and end apart: 1, of which 1 were waited for; matrix products, arithmetic and copies ran while one was open for 0% of the time, Pallas kernels for 0%

commit v1 on v0

v1 whole, which is shorter than its diff:
```python
import functools
import math

import jax
import jax.numpy as jnp
from jax import lax
from jax.experimental import pallas as pl
from jax.experimental.pallas import tpu as pltpu
from jax.sharding import PartitionSpec as P

PCS = 50
ITERS = 4
eps_reg = 0.5
marg_power = 1.0 / (1.0 + eps_reg)
tiny_eps = 1e-06
LN2 = math.log(2.0)
LOG2E = 1.0 / LN2

PAD = 64
BLK = 512
HALF = 16
MESH = pl.DeviceIdType.MESH
f32, bf16 = jnp.float32, jnp.bfloat16


def coords():
    s, t = lax.axis_index("src"), lax.axis_index("tgt")
    return t // 8, (s % 2) * 4 + (t // 2) % 4, s // 2, t % 2


def device(x, y, z, c):
    return (z * 2 + y // 4, (x * 4 + y % 4) * 2 + c)


def split3(v):
    hi = v.astype(bf16)
    rest = v - hi.astype(f32)
    mid = rest.astype(bf16)
    lo = (rest - mid.astype(f32)).astype(bf16)
    return jnp.concatenate([hi, mid, lo], axis=0)


def fold3(v):
    n = v.shape[0] // 3
    return (v[:n] + v[n : 2 * n]) + v[2 * n :]


def logsum_pass(table, shift, out):
    chunk = 64

    def step(n, carry):
        tops, sums = carry
        rows = pl.ds(pl.multiple_of(n * chunk, chunk), chunk)
        moved = shift[rows, :].reshape(chunk // 8, 8, 128)
        new_tops, new_sums = [], []
        for j in range(4):
            v = table[rows, j * 128 : (j + 1) * 128].reshape(chunk // 8, 8, 128) + moved
            top = jnp.maximum(tops[j], jnp.max(v, axis=0))
            total = jnp.sum(jnp.exp2(v - top[None]), axis=0)
            new_sums.append(sums[j] * jnp.exp2(tops[j] - top) + total)
            new_tops.append(top)
        return tuple(new_tops), tuple(new_sums)

    start = (
        tuple(jnp.full((8, 128), -1e30, f32) for _ in range(4)),
        tuple(jnp.zeros((8, 128), f32) for _ in range(4)),
    )
    tops, sums = lax.fori_loop(0, table.shape[0] // chunk, step, start, unroll=2)
    for j in range(4):
        top = jnp.max(tops[j], axis=0, keepdims=True)
        total = jnp.sum(sums[j] * jnp.exp2(tops[j] - top), axis=0, keepdims=True)
        out[pl.ds(j, 1), :] = top + jnp.log2(total)


def potentials(slots, halves, log_mass, log_count):
    v = slots.reshape(-1, 2, 4, 128)
    top = jnp.max(v, axis=0)
    total = top + jnp.log2(jnp.sum(jnp.exp2(v - top[None]), axis=0))
    return marg_power * (log_mass - (total - log_count))


def spread(pot, shift):
    flat = jnp.concatenate([pot[0], pot[1]], axis=0)
    turned = jnp.concatenate([flat, jnp.zeros((120, 128), f32)], axis=0).T
    for p in range(8):
        shift[pl.ds(p * 128, 128), :] = jnp.broadcast_to(turned[:, p : p + 1], (128, 128))


def kernel(
    total_rows, total_cols,
    coupling_hbm, src_hbm, tgt_hbm, smass_hbm, tmass_hbm,
    out_ref, row_ref, col_ref,
    coupling, src_in, tgt_in, src_f, tgt_f, smass, tmass,
    src_t, tgt_t, tgt_two, scores, scores_t, shift,
    m0_s, m0_r, m1_s, m1_r, m2_s, m2_r, row_s, row_r, col_s, col_r,
    load_sem, swap_send, swap_recv, m_send, m_recv, row_send, row_recv, col_send, col_recv,
):
    x, y, z, c = coords()
    yh, yl = y // 4, y % 4

    loads = [
        pltpu.make_async_copy(src_hbm, src_in, load_sem.at[0]),
        pltpu.make_async_copy(tgt_hbm, tgt_in, load_sem.at[1]),
        pltpu.make_async_copy(coupling_hbm, coupling, load_sem.at[2]),
        pltpu.make_async_copy(smass_hbm, smass.at[yh], load_sem.at[3]),
        pltpu.make_async_copy(tmass_hbm, tmass.at[c], load_sem.at[4]),
    ]
    for copy in loads:
        copy.start()

    barrier = pltpu.get_barrier_semaphore()
    greeted = 0
    for dx in range(4):
        for dy in (0, 1, 2, 6, 7):
            for core in range(2):
                if (dx, dy) == (0, 0):
                    if core:
                        continue
                    target = device(x, y, z, 1 - c)
                else:
                    target = device((x + dx) % 4, (y + dy) % 8, z, core)
                pl.semaphore_signal(barrier, inc=1, device_id=target, device_id_type=MESH)
                greeted += 1
    for dy in (3, 4, 5):
        pl.semaphore_signal(barrier, inc=1, device_id=device(x, (y + dy) % 8, z, c), device_id_type=MESH)
        greeted += 1
    for dz in range(1, 8):
        for core in range(2):
            pl.semaphore_signal(barrier, inc=1, device_id=device(x, y, (z + dz) % 8, core), device_id_type=MESH)
            greeted += 1

    for ref, own in ((src_f, yh), (tgt_f, c)):
        ref[own, pl.ds(48, 8), :] = jnp.zeros((8, BLK), f32)
        for side in range(2):
            ref[side, pl.ds(56, 8), :] = jnp.zeros((8, BLK), f32)
    for copy in loads[:2]:
        copy.wait()
    src_f[yh, pl.ds(0, PCS), :] = src_in[...].astype(f32)
    tgt_f[c, pl.ds(0, PCS), :] = tgt_in[...].astype(f32)
    tgt_b = tgt_f[c].astype(bf16)
    tgt_two[pl.ds(0, PAD), :] = tgt_b
    tgt_two[pl.ds(PAD, PAD), :] = tgt_b
    shift[...] = jnp.zeros(shift.shape, f32)
    for copy in loads[2:]:
        copy.wait()

    panel = jnp.dot(src_f[yh].astype(bf16), coupling[...], preferred_element_type=f32)
    wide = lax.dot_general(
        split3(panel), tgt_two[...], (((1,), (1,)), ((), ())), preferred_element_type=f32
    )
    wide = fold3(wide)
    left = lax.broadcasted_iota(jnp.int32, (2 * HALF, 128), 1) < PAD
    packed = jnp.where(left, wide[: 2 * HALF], wide[2 * HALF :])
    m0_s[0] = packed[:HALF]
    m0_s[1] = packed[HALF:]
    m0_r[2 * x + c] = jnp.where(c == 0, packed[:HALF], packed[HALF:])

    pl.semaphore_wait(barrier, greeted)

    def send(src, dst, send_sem, recv_sem, target):
        pltpu.make_async_remote_copy(
            src_ref=src, dst_ref=dst, send_sem=send_sem, recv_sem=recv_sem,
            device_id=target, device_id_type=MESH,
        ).start()

    def settle(ref, sem):
        pltpu.make_async_copy(ref, ref, sem).wait()

    for dx in range(4):
        for half in range(2):
            if dx == 0:
                if half:
                    continue
                send(m0_s.at[1 - c], m0_r.at[2 * x + c], m_send.at[0], m_recv.at[0], device(x, y, z, 1 - c))
            else:
                send(m0_s.at[half], m0_r.at[2 * x + c], m_send.at[0], m_recv.at[0], device((x + dx) % 4, y, z, half))

    other = device(x, y, z, 1 - c)
    send(tgt_f.at[c, pl.ds(0, 56)], tgt_f.at[c, pl.ds(0, 56)], swap_send.at[0], swap_recv.at[0], other)
    send(tmass.at[c], tmass.at[c], swap_send.at[1], swap_recv.at[1], other)
    way = jnp.where(yl == 3, 1, 7)

    @pl.when((yl == 0) | (yl == 3))
    def _():
        for far in range(1, 3):
            target = device(x, (y + far * way) % 8, z, c)
            send(src_f.at[yh, pl.ds(0, 56)], src_f.at[yh, pl.ds(0, 56)], swap_send.at[1 + 2 * far - 1], swap_recv.at[2], target)
            send(smass.at[yh], smass.at[yh], swap_send.at[1 + 2 * far], swap_recv.at[3], target)

    settle(m0_r.at[pl.ds(0, 7)], m_recv.at[0])
    part = jnp.sum(m0_r[...], axis=0)
    m1_s[...] = part
    m1_r[y] = part
    for dy in range(1, 8):
        send(m1_s, m1_r.at[y], m_send.at[1], m_recv.at[1], device(x, (y + dy) % 8, z, c))

    settle(tgt_f.at[0, pl.ds(0, 56)], swap_recv.at[0])
    settle(tmass.at[0], swap_recv.at[1])
    zero = jnp.zeros((PAD, BLK), f32)
    for core in range(2):
        rows = tgt_f[core]
        tgt_t[pl.ds(core * BLK, BLK), :] = jnp.concatenate([rows, rows, rows, zero], axis=0).T.astype(bf16)

    settle(m1_r.at[pl.ds(0, 7)], m_recv.at[1])
    part = jnp.sum(m1_r[...], axis=0)
    m2_s[...] = part
    m2_r[2 * z + c] = part
    for dz in range(8):
        for core in range(2):
            if dz == 0:
                if core:
                    continue
                target = other
            else:
                target = device(x, y, (z + dz) % 8, core)
            send(m2_s, m2_r.at[2 * z + c], m_send.at[2], m_recv.at[2], target)

    settle(src_f.at[0, pl.ds(0, 56)], swap_recv.at[2])
    settle(smass.at[0], swap_recv.at[3])
    for side in range(2):
        rows = src_f[side]
        src_t[pl.ds(side * BLK, BLK), :] = jnp.concatenate([rows, rows, rows, zero], axis=0).T.astype(bf16)
    log_src = jnp.log2(smass[...])
    log_tgt = jnp.log2(tmass[...])

    settle(m2_r.at[pl.ds(0, 15)], m_recv.at[2])
    sums = jnp.sum(m2_r[...].reshape(8, 2, HALF, 128), axis=0)
    moment = jnp.concatenate([sums[0], sums[1]], axis=0) * (total_rows * total_cols) ** (-0.5)
    square = jnp.sum(moment * moment, axis=1, keepdims=True)
    square = jnp.sum(square, axis=0, keepdims=True) * (1.0 / (PCS * PCS))
    normed = moment / jnp.sqrt(square + tiny_eps) * (2.0 / (eps_reg * PCS) * LOG2E)

    two = jnp.concatenate([jnp.where(left, normed, 0.0), jnp.where(left, 0.0, normed)], axis=0)
    turned = jnp.concatenate([two, jnp.zeros((PAD, 128), f32)], axis=0).T
    back = turned[:PAD, :PAD] + turned[PAD:, :PAD]
    fill = jnp.zeros((PAD, BLK), bf16)
    weighted = fold3(jnp.dot(split3(two), tgt_two[...], preferred_element_type=f32))
    weighted = jnp.concatenate([split3(weighted), fill], axis=0)
    mine = src_f[c].astype(bf16)
    weighted_t = fold3(jnp.dot(split3(back), mine, preferred_element_type=f32))
    weighted_t = jnp.concatenate([split3(weighted_t), fill], axis=0)
    for n in range(8):
        rows = pl.ds(n * 128, 128)
        scores_t[rows, :] = jnp.dot(tgt_t[rows, :], weighted_t, preferred_element_type=f32)
    for n in range(8):
        rows = pl.ds(n * 128, 128)
        scores[rows, :] = jnp.dot(src_t[rows, :], weighted, preferred_element_type=f32)

    row_slot = 2 * (4 * x + yl) + c
    col_slot = 2 * z + c
    y_two = (y + 2 + 4 * (x % 2)) % 8
    log_rows, log_cols = math.log2(total_rows), math.log2(total_cols)

    def iteration(it, _):
        logsum_pass(scores_t, shift, row_s.at[it])
        row_r[it, row_slot] = row_s[it]
        for dx in range(4):
            for ty in (y, (y + 1) % 8, (y + 7) % 8, y_two):
                for core in range(2):
                    if dx == 0 and ty is y:
                        if core:
                            continue
                        target = other
                    else:
                        target = device((x + dx) % 4, ty, z, core)
                    send(row_s.at[it], row_r.at[it, row_slot], row_send.at[it], row_recv.at[it], target)
        settle(row_r.at[it, pl.ds(0, 31)], row_recv.at[it])
        row_pot = potentials(row_r[it], 16, log_src, log_cols)
        spread(row_pot, shift)
        row_ref[...] = jnp.where(yh == 0, row_pot[0], row_pot[1]) * LN2

        logsum_pass(scores, shift, col_s.at[it])
        col_r[it, col_slot] = col_s[it]
        for dz in range(8):
            for core in range(2):
                if dz == 0:
                    if core:
                        continue
                    target = other
                else:
                    target = device(x, y, (z + dz) % 8, core)
                send(col_s.at[it], col_r.at[it, col_slot], col_send.at[it], col_recv.at[it], target)
        settle(col_r.at[it, pl.ds(0, 15)], col_recv.at[it])
        col_pot = potentials(col_r[it], 8, log_tgt, log_rows)
        col_ref[...] = jnp.where(c == 0, col_pot[0], col_pot[1])

        @pl.when(it == ITERS - 1)
        def _():
            for j in range(4):
                lanes = pl.ds(j * 128, 128)
                add = col_ref[pl.ds(j, 1), :]
                for n in range(8):
                    rows = pl.ds(pl.multiple_of(yh * BLK + n * 64, 64), 64)
                    out_ref[pl.ds(n * 64, 64), lanes] = ((scores[rows, lanes] + shift[rows, :]) + add) * LN2

        spread(col_pot, shift)
        col_ref[...] = col_ref[...] * LN2
        return 0

    lax.fori_loop(0, ITERS, iteration, 0)

    settle(m0_r.at[pl.ds(0, 7)], m_send.at[0])
    settle(m1_r.at[pl.ds(0, 7)], m_send.at[1])
    settle(m2_r.at[pl.ds(0, 15)], m_send.at[2])
    settle(tgt_f.at[0, pl.ds(0, 56)], swap_send.at[0])
    settle(tmass.at[0], swap_send.at[1])

    @pl.when((yl == 0) | (yl == 3))
    def _():
        for far in range(1, 3):
            settle(src_f.at[0, pl.ds(0, 56)], swap_send.at[1 + 2 * far - 1])
            settle(smass.at[0], swap_send.at[1 + 2 * far])

    for it in range(ITERS):
        settle(row_r.at[it, pl.ds(0, 31)], row_send.at[it])
        settle(col_r.at[it, pl.ds(0, 15)], col_send.at[it])


def shards(coupling, src_pcs, tgt_pcs, src_mass, tgt_mass):
    total_rows = coupling.shape[0] * lax.axis_size("src")
    total_cols = coupling.shape[1] * lax.axis_size("tgt")
    dma = pltpu.SemaphoreType.DMA
    vec = lambda *lead: pltpu.VMEM((*lead, 4, 128), f32)
    out, row, col = pl.pallas_call(
        functools.partial(kernel, total_rows, total_cols),
        out_shape=(
            jax.ShapeDtypeStruct((BLK, BLK), f32),
            jax.ShapeDtypeStruct((4, 128), f32),
            jax.ShapeDtypeStruct((4, 128), f32),
        ),
        in_specs=[pl.BlockSpec(memory_space=pl.ANY)] * 5,
        out_specs=[pl.BlockSpec(memory_space=pltpu.VMEM)] * 3,
        scratch_shapes=[
            pltpu.VMEM((BLK, BLK), bf16),
            pltpu.VMEM((PCS, BLK), bf16),
            pltpu.VMEM((PCS, BLK), bf16),
            pltpu.VMEM((2, PAD, BLK), f32),
            pltpu.VMEM((2, PAD, BLK), f32),
            vec(2),
            vec(2),
            pltpu.VMEM((2 * BLK, 4 * PAD), bf16),
            pltpu.VMEM((2 * BLK, 4 * PAD), bf16),
            pltpu.VMEM((2 * PAD, BLK), bf16),
            pltpu.VMEM((2 * BLK, BLK), f32),
            pltpu.VMEM((2 * BLK, BLK), f32),
            pltpu.VMEM((2 * BLK, 128), f32),
            pltpu.VMEM((2, HALF, 128), f32),
            pltpu.VMEM((8, HALF, 128), f32),
            pltpu.VMEM((HALF, 128), f32),
            pltpu.VMEM((8, HALF, 128), f32),
            pltpu.VMEM((HALF, 128), f32),
            pltpu.VMEM((16, HALF, 128), f32),
            vec(ITERS),
            vec(ITERS, 32),
            vec(ITERS),
            vec(ITERS, 16),
            dma((5,)),
            dma((6,)),
            dma((4,)),
            dma((3,)),
            dma((3,)),
            dma((ITERS,)),
            dma((ITERS,)),
            dma((ITERS,)),
            dma((ITERS,)),
        ],
        compiler_params=pltpu.CompilerParams(collective_id=0, has_side_effects=True),
        name="coupling_step",
    )(coupling, src_pcs, tgt_pcs, src_mass.reshape(4, 128), tgt_mass.reshape(4, 128))
    return out, row.reshape(-1), col.reshape(-1)


def solution(mesh):
    in_specs = (P("src", "tgt"), P(None, "src"), P(None, "tgt"), P("src"), P("tgt"))
    out_specs = (P("src", "tgt"), P("src"), P("tgt"))
    return jax.shard_map(shards, mesh=mesh, in_specs=in_specs, out_specs=out_specs, check_vma=False)
```

time: 1300 us -> 85.1 us (0.07); the launches traced: 1290 us -> 84.9 us
  blocking collectives: 1060 us -> 0 us
  waiting for transfers between devices: 195 us -> 0 us
  Pallas kernels: 0 us -> 80.7 us
  between operations: 14.8 us -> 0.65 us
    psum x9 -> x0, blocking collectives: 580 us -> none  [the longest x4 269 us: row_logmean(): lax.psum(jnp.sum(jnp.exp(shifted - highest[:, None]), axis=1), 'tgt')]
    pmax x8 -> x0, blocking collectives: 485 us -> none  [the longest x4 318 us: row_logmean(): highest = lax.pmax(local_max, 'tgt')]
    psum x1 -> x0, waiting for transfers between devices: 195 us -> none  [shards(): summed_panel = lax.psum(partial_cols, 'src')]
    pallas_call x0 -> x1, Pallas kernels: none -> 80.7 us  [shards(): pl.pallas_call(functools.partial(kernel, total_rows, total_cols), out_sha...]
  transfers between devices with their start and end apart: 1 -> 0, of which waited for: 1 -> 0; matrix products, arithmetic and copies ran while one was open for 0% -> 0% of each run, Pallas kernels for 0% -> 0%
where the time goes in v1:
time: 85.1 us; the launch traced here: 84.9 us
  Pallas kernels  80.7 us (95%)
  local copies, waits for them, and re-layouts  3.52 us (4%)
    pallas_call x1, Pallas kernels, shards(): pl.pallas_call(functools.partial(kernel, total_rows, total_cols), out_sha...  80.7 us
    unnamed x7, local copies, waits for them, and re-layouts  3.52 us

profile of v1, /device:TPU:1, one launch (start us, length us, event | category | flops | bytes accessed | tf_op | source)
XLA Modules:
  0.0 84.9 jit_solution(14687399298240760630)
XLA Ops:
  0.6 80.7 %coupling_step.1 = (f32[512,512]{1,0:T(8,128)}, f32[4,128]{1,0:T(4,128)}, f32[4,128]{1,0:T(4,128)}) custom-call(bf16[512,512]{1,0:T(8,128)(2,1)} %coupling_hbm.1, bf16[50,512]{1,0:T(8,128)(2,1)} %src_hbm.1, bf16[50,512]{1,0:T(8,128)(2,1)} %tgt_hbm.1, f32[4,128]{1,0:T(4,128)} %bitcast.4, f32[4,128]{1,0:T(4,128)} %bitcast.5), custom_call_target="tpu_custom_call" | custom-call | tf_op jit(solution)/shard_map/coupling_step/pallas_call | solution.py:324
  81.4 0.0 copy-start.1
  81.4 2.3 %copy.11 = f32[512,512]{1,0:T(8,128)} copy(f32[512,512]{1,0:T(8,128)} %get-tuple-element.12) | data formatting | bytes 2097152
  83.7 0.0 copy-done.1
  83.7 0.0 copy-start
  83.7 0.6 copy.12
  84.2 0.1 copy-done
  84.3 0.6 copy.13
Async XLA Ops:
  81.4 2.3 %copy-start.1 = (f32[4,128]{1,0:T(4,128)S(1)}, f32[4,128]{1,0:T(4,128)}, u32[]{:S(2)}) copy-start(f32[4,128]{1,0:T(4,128)} %get-tuple-element.7) | copy-start | bytes 6148
  83.7 0.7 copy-start

commit v2 on v0

v2 whole, which is shorter than its diff:
```python
import functools
import math

import jax
import jax.numpy as jnp
from jax import lax
from jax.experimental import pallas as pl
from jax.experimental.pallas import tpu as pltpu
from jax.sharding import PartitionSpec as P

PCS = 50
ITERS = 4
eps_reg = 0.5
marg_power = 1.0 / (1.0 + eps_reg)
tiny_eps = 1e-06
LN2 = math.log(2.0)
LOG2E = 1.0 / LN2

PAD = 64
SENT = 56
BLK = 512
TWO = 2 * BLK
MESH = pl.DeviceIdType.MESH
f32, bf16 = jnp.float32, jnp.bfloat16
FAR_X, FAR_8 = (2, 1, 3), (4, 3, 5, 2, 6, 1, 7)


def coords():
    s, t = lax.axis_index("src"), lax.axis_index("tgt")
    return t // 8, (s % 2) * 4 + (t // 2) % 4, s // 2, t % 2


def device(x, y, z, c):
    return (z * 2 + y // 4, (x * 4 + y % 4) * 2 + c)


def split3(v):
    hi = v.astype(bf16)
    rest = v - hi.astype(f32)
    mid = rest.astype(bf16)
    lo = (rest - mid.astype(f32)).astype(bf16)
    return jnp.concatenate([hi, mid, lo], axis=0)


def fold3(v):
    n = v.shape[0] // 3
    return (v[:n] + v[n : 2 * n]) + v[2 * n :]


def thrice(v):
    return jnp.concatenate([v, v, v, jnp.zeros_like(v)], axis=0).T.astype(bf16)


def stack4(v):
    terms = split3(v)
    return jnp.concatenate([terms, jnp.zeros((PAD, v.shape[1]), bf16)], axis=0)


def turn(pot):
    return jnp.concatenate([pot, jnp.zeros((120, 128), f32)], axis=0).T


def logsum_pass(table, pot, shift, out):
    turned = turn(pot)
    for pair in range(4):
        tops = [jnp.full((8, 128), -1e30, f32)] * 2
        sums = [jnp.zeros((8, 128), f32)] * 2
        for p in range(8):
            rows = pl.ds(p * 128, 128)
            if pair == 0:
                moved = jnp.broadcast_to(turned[:, p : p + 1], (128, 128))
                shift[rows, :] = moved
            else:
                moved = shift[rows, :]
            moved = moved.reshape(16, 8, 128)
            for k in range(2):
                j = 2 * pair + k
                v = table[rows, j * 128 : (j + 1) * 128].reshape(16, 8, 128) + moved
                top = jnp.maximum(tops[k], jnp.max(v, axis=0))
                total = jnp.sum(jnp.exp2(v - top[None]), axis=0)
                sums[k] = sums[k] * jnp.exp2(tops[k] - top) + total
                tops[k] = top
        for k in range(2):
            top = jnp.max(tops[k], axis=0, keepdims=True)
            total = jnp.sum(sums[k] * jnp.exp2(tops[k] - top), axis=0, keepdims=True)
            out[pl.ds(2 * pair + k, 1), :] = top + jnp.log2(total)


def potentials(v, log_mass, log_count):
    top = jnp.max(v, axis=0)
    total = top + jnp.log2(jnp.sum(jnp.exp2(v - top[None]), axis=0))
    return marg_power * (log_mass - (total - log_count))


def send(src, dst, send_sem, recv_sem, target):
    pltpu.make_async_remote_copy(
        src_ref=src, dst_ref=dst, send_sem=send_sem, recv_sem=recv_sem,
        device_id=target, device_id_type=MESH,
    ).start()


def settle(ref, sem):
    pltpu.make_async_copy(ref, ref, sem).wait()


def greet(targets):
    barrier = pltpu.get_barrier_semaphore()
    for target in targets:
        pl.semaphore_signal(barrier, inc=1, device_id=target, device_id_type=MESH)


def kernel(
    total_rows, total_cols,
    coupling_hbm, src_hbm, tgt_hbm, smass_hbm, tmass_hbm,
    sum_ref, row_ref, col_ref,
    coupling, src_in, tgt_in, src_b, tgt_two, src_f, tgt_f, smass, tmass,
    src_t, tgt_t, src_all, tgt_all, scores, scores_t, shift, pot,
    m0_s, m0_r, m1_s, m1_r, m2_s, m2_r, nrm, row_s, row_r, col_s, col_r, fin_s,
    load_sem, swap_send, swap_recv, m_send, m_recv, row_send, row_recv, col_send, col_recv, fin_send, fin_recv,
):
    x, y, z, c = coords()
    yh, yl = y // 4, y % 4
    on_one, on_zero = c == 1, c == 0

    loads = [
        pltpu.make_async_copy(src_hbm, src_in, load_sem.at[0]),
        pltpu.make_async_copy(tgt_hbm, tgt_in, load_sem.at[1]),
        pltpu.make_async_copy(coupling_hbm, coupling, load_sem.at[2]),
        pltpu.make_async_copy(smass_hbm, smass.at[yh], load_sem.at[3]),
        pltpu.make_async_copy(tmass_hbm, tmass.at[c], load_sem.at[4]),
    ]
    for copy in loads:
        copy.start()

    row_peers = [(dx, dy) for dx in (2, 1, 3, 0) for dy in (2, 6, 1, 7)]
    ones = [device((x + dx) % 4, (y + dy) % 8, z, 1) for dx, dy in row_peers]
    ones += [device((x + dx) % 4, y, z, 1) for dx in FAR_X]
    ones += [device(x, (y + dy) % 8, z, 1) for dy in (4, 3, 5)]
    ones += [device(x, y, (z + dz) % 8, 1) for dz in FAR_8]
    near = [device((x + dx) % 4, y, z, 0) for dx in (2, 1, 3, 0)]

    @pl.when(on_one)
    def _():
        greet(ones + near)

    @pl.when(on_zero)
    def _():
        greet([device(x, y, (z + dz) % 8, 1) for dz in FAR_8])
        greet([device((x + dx) % 4, y, z, 1) for dx in (2, 1, 3, 0)])

    src_b[pl.ds(48, 16), :] = jnp.zeros((16, BLK), bf16)
    tgt_two[pl.ds(48, 16), :] = jnp.zeros((16, BLK), bf16)
    tgt_two[pl.ds(112, 16), :] = jnp.zeros((16, BLK), bf16)
    for copy in loads[:2]:
        copy.wait()
    src_b[pl.ds(0, PCS), :] = src_in[...]
    tgt_two[pl.ds(0, PCS), :] = tgt_in[...]
    tgt_two[pl.ds(PAD, PCS), :] = tgt_in[...]
    loads[2].wait()

    panel = jnp.dot(src_b[...], coupling[...], preferred_element_type=f32)
    wide = fold3(
        lax.dot_general(
            split3(panel), tgt_two[...], (((1,), (1,)), ((), ())), preferred_element_type=f32
        )
    )
    left = lax.broadcasted_iota(jnp.int32, (32, 128), 1) < PAD
    packed = jnp.where(left, wide[:32], wide[32:])
    m0_s[...] = packed

    barrier = pltpu.get_barrier_semaphore()
    own0 = 2 * x + c

    @pl.when(on_one)
    def _():
        pl.semaphore_wait(barrier, len(ones) + 7 + 4)
        m0_r[own0] = packed
        for dx in FAR_X:
            send(m0_s, m0_r.at[own0], m_send.at[0], m_recv.at[0], device((x + dx) % 4, y, z, 1))

    @pl.when(on_zero)
    def _():
        pl.semaphore_wait(barrier, 4)
        for dx in (2, 1, 3, 0):
            send(m0_s, m0_r.at[own0], m_send.at[0], m_recv.at[0], device((x + dx) % 4, y, z, 1))

    for ref, own, block in ((src_f, yh, src_b), (tgt_f, c, tgt_two)):
        for side in range(2):
            ref[side, pl.ds(SENT, 8), :] = jnp.zeros((8, BLK), f32)
        ref[own, pl.ds(0, SENT), :] = block[pl.ds(0, PAD), :].astype(f32)[:SENT]
    for copy in loads[3:]:
        copy.wait()

    rows56 = pl.ds(0, SENT)

    def normed_of(packed_sum):
        moment = packed_sum * (total_rows * total_cols) ** (-0.5)
        square = jnp.sum(moment * moment, axis=1, keepdims=True)
        square = jnp.sum(square, axis=0, keepdims=True) * (1.0 / (PCS * PCS))
        scaled = moment / jnp.sqrt(square + tiny_eps) * (2.0 / (eps_reg * PCS) * LOG2E)
        return jnp.concatenate([jnp.where(left, scaled, 0.0), jnp.where(left, 0.0, scaled)], axis=0)

    log_rows, log_cols = math.log2(total_rows), math.log2(total_cols)
    partner = device(x, y, z, 1 - c)
    last = ITERS - 1

    @pl.when(on_zero)
    def _():
        send(tgt_f.at[0, rows56], tgt_f.at[0, rows56], swap_send.at[0], swap_recv.at[0], partner)
        send(tmass.at[0], tmass.at[0], swap_send.at[1], swap_recv.at[1], partner)
        src_t[pl.ds(0, BLK), :] = thrice(src_f[yh])
        log_tgt = jnp.log2(tmass[0])

        settle(nrm, fin_recv.at[0])
        weighted = fold3(jnp.dot(split3(normed_of(nrm[...])), tgt_two[...], preferred_element_type=f32))
        sum_ref[...] = jnp.dot(src_t[pl.ds(0, BLK), :], stack4(weighted), preferred_element_type=f32)

        settle(pot, fin_recv.at[1])
        half = jnp.where(yh == 0, pot[pl.ds(0, 4), :], pot[pl.ds(4, 4), :])
        row_ref[...] = half * LN2
        turned = turn(jnp.concatenate([half, jnp.zeros((4, 128), f32)], axis=0))
        for p in range(4):
            rows = pl.ds(p * 128, 128)
            moved = jnp.broadcast_to(turned[:, p : p + 1], (128, 128))
            for j in range(4):
                lanes = pl.ds(j * 128, 128)
                sum_ref[rows, lanes] = sum_ref[rows, lanes] + moved

        settle(col_r.at[last], col_recv.at[last])
        col_ref[...] = potentials(col_r[last][:, :4, :], log_tgt, log_rows)

        settle(m0_r.at[pl.ds(0, 4)], m_send.at[0])
        settle(tgt_f.at[0, rows56], swap_send.at[0])
        settle(tmass.at[0], swap_send.at[1])

    edge = (yl == 0) | (yl == 3)

    @pl.when(on_one & edge)
    def _():
        way = jnp.where(yl == 3, 1, 7)
        for far in range(1, 3):
            target = device(x, (y + far * way) % 8, z, 1)
            send(src_f.at[yh, rows56], src_f.at[yh, rows56], swap_send.at[2 * far - 2], swap_recv.at[2], target)
            send(smass.at[yh], smass.at[yh], swap_send.at[2 * far - 1], swap_recv.at[3], target)

    @pl.when(on_one)
    def _():
        tgt_t[pl.ds(BLK, BLK), :] = thrice(tgt_f[1])

        settle(m0_r.at[pl.ds(0, 7)], m_recv.at[0])
        part = jnp.sum(m0_r[...], axis=0)
        m1_s[...] = part
        for dy in FAR_8:
            send(m1_s, m1_r.at[y], m_send.at[1], m_recv.at[1], device(x, (y + dy) % 8, z, 1))
        m1_r[y] = part

        settle(tgt_f.at[0, rows56], swap_recv.at[0])
        settle(tmass.at[0], swap_recv.at[1])
        tgt_t[pl.ds(0, BLK), :] = thrice(tgt_f[0])
        near_b = tgt_f[0].astype(bf16)
        tgt_all[pl.ds(0, PAD), pl.ds(0, BLK)] = near_b
        tgt_all[pl.ds(PAD, PAD), pl.ds(0, BLK)] = near_b
        tgt_all[:, pl.ds(BLK, BLK)] = tgt_two[...]

        settle(m1_r.at[pl.ds(0, 7)], m_recv.at[1])
        part = jnp.sum(m1_r[...], axis=0)
        m2_s[...] = part
        for dz in FAR_8:
            send(m2_s, m2_r.at[z], m_send.at[2], m_recv.at[2], device(x, y, (z + dz) % 8, 1))
        m2_r[z] = part

        settle(src_f.at[0, rows56], swap_recv.at[2])
        settle(smass.at[0], swap_recv.at[3])
        for side in range(2):
            src_t[pl.ds(side * BLK, BLK), :] = thrice(src_f[side])
            src_all[:, pl.ds(side * BLK, BLK)] = src_f[side].astype(bf16)
        log_src = jnp.log2(jnp.concatenate([smass[0], smass[1]], axis=0))
        log_tgt = jnp.log2(jnp.concatenate([tmass[0], tmass[1]], axis=0))
        pot[...] = jnp.zeros((8, 128), f32)

        settle(m2_r.at[pl.ds(0, 7)], m_recv.at[2])
        total = jnp.sum(m2_r[...], axis=0)
        nrm[...] = total
        send(nrm, nrm, fin_send.at[0], fin_recv.at[0], partner)

        two = normed_of(total)
        turned = jnp.concatenate([two, jnp.zeros((PAD, 128), f32)], axis=0).T
        back = turned[:PAD, :PAD] + turned[PAD:, :PAD]
        weighted_t = stack4(fold3(jnp.dot(split3(back), src_all[...], preferred_element_type=f32)))
        for n in range(8):
            rows = pl.ds(n * 128, 128)
            scores_t[rows, :] = jnp.dot(tgt_t[rows, :], weighted_t, preferred_element_type=f32)

        row_slot = 4 * x + yl
        y_two = (y + 2 + 4 * (x % 2)) % 8

        def iteration(it, _):
            logsum_pass(scores_t, pot[...], shift, row_s.at[it])
            for dx in (2, 1, 3, 0):
                for ty in (y_two, (y + 1) % 8, (y + 7) % 8, y):
                    if dx or ty is not y:
                        target = device((x + dx) % 4, ty, z, 1)
                        send(row_s.at[it], row_r.at[it, row_slot], row_send.at[it], row_recv.at[it], target)
            row_r[it, row_slot] = row_s[it]

            @pl.when(it == 0)
            def _():
                weighted = stack4(fold3(jnp.dot(split3(two), tgt_all[...], preferred_element_type=f32)))
                for n in range(8):
                    rows = pl.ds(n * 128, 128)
                    scores[rows, :] = jnp.dot(src_t[rows, :], weighted, preferred_element_type=f32)

            settle(row_r.at[it, pl.ds(0, 15)], row_recv.at[it])
            row_pot = potentials(row_r[it], log_src, log_cols)
            pot[...] = row_pot

            @pl.when(it == last)
            def _():
                fin_s[...] = row_pot
                send(fin_s, pot, fin_send.at[1], fin_recv.at[1], partner)

            logsum_pass(scores, row_pot, shift, col_s.at[it])
            for dz in FAR_8:
                send(col_s.at[it], col_r.at[it, z], col_send.at[it], col_recv.at[it], device(x, y, (z + dz) % 8, 1))
            col_r[it, z] = col_s[it]

            @pl.when(it == last)
            def _():
                for dz in (*FAR_8, 0):
                    target = device(x, y, (z + dz) % 8, 0)
                    send(col_s.at[it], col_r.at[it, z], fin_send.at[2], col_recv.at[it], target)
                row_ref[...] = jnp.where(yh == 0, row_pot[:4], row_pot[4:]) * LN2
                for n in range(4):
                    to = pl.ds(n * 128, 128)
                    rows = pl.ds(pl.multiple_of(yh * BLK + n * 128, 128), 128)
                    moved = shift[rows, :]
                    for j in range(4):
                        sum_ref[to, pl.ds(j * 128, 128)] = scores[rows, pl.ds(BLK + j * 128, 128)] + moved

            settle(col_r.at[it, pl.ds(0, 7)], col_recv.at[it])
            pot[...] = potentials(col_r[it], log_tgt, log_rows)
            return 0

        lax.fori_loop(0, ITERS, iteration, 0)
        col_ref[...] = pot[pl.ds(4, 4), :]

        settle(m0_r.at[pl.ds(0, 3)], m_send.at[0])
        settle(m1_r.at[pl.ds(0, 7)], m_send.at[1])
        settle(m2_r.at[pl.ds(0, 7)], m_send.at[2])
        settle(nrm, fin_send.at[0])
        settle(fin_s, fin_send.at[1])
        settle(col_r.at[last], fin_send.at[2])
        for it in range(ITERS):
            settle(row_r.at[it, pl.ds(0, 15)], row_send.at[it])
            settle(col_r.at[it, pl.ds(0, 7)], col_send.at[it])

    @pl.when(on_one & edge)
    def _():
        for far in range(1, 3):
            settle(src_f.at[0, rows56], swap_send.at[2 * far - 2])
            settle(smass.at[0], swap_send.at[2 * far - 1])


def finish(sum_ref, row_in, col_in, out_hbm, row_ref, col_ref, tile, sem):
    copies = []
    for n in range(8):
        rows = pl.ds(n * 64, 64)
        for j in range(4):
            lanes = pl.ds(j * 128, 128)
            tile[rows, lanes] = (sum_ref[rows, lanes] + col_in[pl.ds(j, 1), :]) * LN2
        copies.append(pltpu.make_async_copy(tile.at[rows], out_hbm.at[rows], sem.at[n]))
        copies[-1].start()
    row_ref[...] = row_in[...]
    col_ref[...] = col_in[...] * LN2
    for copy in copies:
        copy.wait()


def shards(coupling, src_pcs, tgt_pcs, src_mass, tgt_mass):
    total_rows = coupling.shape[0] * lax.axis_size("src")
    total_cols = coupling.shape[1] * lax.axis_size("tgt")
    dma = pltpu.SemaphoreType.DMA
    full, vec = jax.ShapeDtypeStruct((BLK, BLK), f32), jax.ShapeDtypeStruct((4, 128), f32)
    in_vmem, anywhere = pl.BlockSpec(memory_space=pltpu.VMEM), pl.BlockSpec(memory_space=pl.ANY)
    tile = lambda *lead: pltpu.VMEM((*lead, 8, 128), f32)
    gram = lambda *lead: pltpu.VMEM((*lead, 32, 128), f32)
    sums, row, col = pl.pallas_call(
        functools.partial(kernel, total_rows, total_cols),
        out_shape=(full, vec, vec),
        in_specs=[anywhere] * 5,
        out_specs=[in_vmem] * 3,
        scratch_shapes=[
            pltpu.VMEM((BLK, BLK), bf16),
            pltpu.VMEM((PCS, BLK), bf16),
            pltpu.VMEM((PCS, BLK), bf16),
            pltpu.VMEM((PAD, BLK), bf16),
            pltpu.VMEM((2 * PAD, BLK), bf16),
            pltpu.VMEM((2, PAD, BLK), f32),
            pltpu.VMEM((2, PAD, BLK), f32),
            pltpu.VMEM((2, 4, 128), f32),
            pltpu.VMEM((2, 4, 128), f32),
            pltpu.VMEM((TWO, 4 * PAD), bf16),
            pltpu.VMEM((TWO, 4 * PAD), bf16),
            pltpu.VMEM((PAD, TWO), bf16),
            pltpu.VMEM((2 * PAD, TWO), bf16),
            pltpu.VMEM((TWO, TWO), f32),
            pltpu.VMEM((TWO, TWO), f32),
            pltpu.VMEM((TWO, 128), f32),
            tile(),
            gram(),
            gram(8),
            gram(),
            gram(8),
            gram(),
            gram(8),
            gram(),
            tile(ITERS),
            tile(ITERS, 16),
            tile(ITERS),
            tile(ITERS, 8),
            tile(),
            dma((5,)),
            dma((4,)),
            dma((4,)),
            dma((3,)),
            dma((3,)),
            dma((ITERS,)),
            dma((ITERS,)),
            dma((ITERS,)),
            dma((ITERS,)),
            dma((3,)),
            dma((3,)),
        ],
        compiler_params=pltpu.CompilerParams(collective_id=0, has_side_effects=True),
        name="coupling_step",
    )(coupling, src_pcs, tgt_pcs, src_mass.reshape(4, 128), tgt_mass.reshape(4, 128))
    out, row, col = pl.pallas_call(
        finish,
        out_shape=(full, vec, vec),
        in_specs=[in_vmem] * 3,
        out_specs=[anywhere, in_vmem, in_vmem],
        scratch_shapes=[pltpu.VMEM((BLK, BLK), f32), dma((8,))],
        name="finish",
    )(sums, row, col)
    return out, row.reshape(-1), col.reshape(-1)


def solution(mesh):
    in_specs = (P("src", "tgt"), P(None, "src"), P(None, "tgt"), P("src"), P("tgt"))
    out_specs = (P("src", "tgt"), P("src"), P("tgt"))
    return jax.shard_map(shards, mesh=mesh, in_specs=in_specs, out_specs=out_specs, check_vma=False)
```

time: 1300 us -> 71.5 us (0.06); the launches traced: 1290 us -> 71.4 us
  blocking collectives: 1060 us -> 0 us
  waiting for transfers between devices: 195 us -> 0 us
  Pallas kernels: 0 us -> 70.7 us
  between operations: 14.8 us -> 0.64 us
    psum x9 -> x0, blocking collectives: 580 us -> none  [the longest x4 269 us: row_logmean(): lax.psum(jnp.sum(jnp.exp(shifted - highest[:, None]), axis=1), 'tgt')]
    pmax x8 -> x0, blocking collectives: 485 us -> none  [the longest x4 318 us: row_logmean(): highest = lax.pmax(local_max, 'tgt')]
    psum x1 -> x0, waiting for transfers between devices: 195 us -> none  [shards(): summed_panel = lax.psum(partial_cols, 'src')]
    pallas_call x0 -> x2, Pallas kernels: none -> 70.7 us  [the longest x1 67.9 us: shards(): pl.pallas_call(functools.partial(kernel, total_rows, total_cols), out_sha...]
  transfers between devices with their start and end apart: 1 -> 0, of which waited for: 1 -> 0; matrix products, arithmetic and copies ran while one was open for 0% -> 0% of each run, Pallas kernels for 0% -> 0%
where the time goes in v2:
time: 71.5 us; the launch traced here: 71.4 us
  Pallas kernels  70.7 us (99%)
    pallas_call x1, Pallas kernels, shards(): pl.pallas_call(functools.partial(kernel, total_rows, total_cols), out_sha...  67.9 us
    pallas_call x1, Pallas kernels, shards(): pl.pallas_call(finish, out_shape=(full, vec, vec), in_specs=[in_vmem] * 3...  2.85 us

profile of v2, /device:TPU:1, one launch (start us, length us, event | category | flops | bytes accessed | tf_op | source)
XLA Modules:
  0.0 71.4 jit_solution(3767623218556359283)
XLA Ops:
  0.6 67.9 %coupling_step.1 = (f32[512,512]{1,0:T(8,128)}, f32[4,128]{1,0:T(4,128)}, f32[4,128]{1,0:T(4,128)}) custom-call(bf16[512,512]{1,0:T(8,128)(2,1)} %coupling_hbm.1, bf16[50,512]{1,0:T(8,128)(2,1)} %src_hbm.1, bf16[50,512]{1,0:T(8,128)(2,1)} %tgt_hbm.1, f32[4,128]{1,0:T(4,128)} %bitcast.4, f32[4,128]{1,0:T(4,128)} %bitcast.5), custom_call_target="tpu_custom_call" | custom-call | tf_op jit(solution)/shard_map/coupling_step/pallas_call | solution.py:387
  68.5 2.9 %finish.1 = (f32[512,512]{1,0:T(8,128)}, f32[4,128]{1,0:T(4,128)}, f32[4,128]{1,0:T(4,128)}) custom-call(f32[512,512]{1,0:T(8,128)} %get-tuple-element.9.sum_ref, f32[4,128]{1,0:T(4,128)} %get-tuple-element.10.row_in, f32[4,128]{1,0:T(4,128)} %get-tuple-element.11.col_in), custom_call_target="tpu_custom_call" | custom-call | tf_op jit(solution)/shard_map/finish/pallas_call | solution.py:437

commit v3 on v2

--- a/solution.py
+++ b/solution.py
@@ -386,7 +386,7 @@
     gram = lambda *lead: pltpu.VMEM((*lead, 32, 128), f32)
     sums, row, col = pl.pallas_call(
         functools.partial(kernel, total_rows, total_cols),
-        out_shape=(full, vec, vec),
+        out_shape=(pltpu.VMEM((BLK, BLK), f32), pltpu.VMEM((4, 128), f32), pltpu.VMEM((4, 128), f32)),
         in_specs=[anywhere] * 5,
         out_specs=[in_vmem] * 3,
         scratch_shapes=[
@@ -440,8 +440,9 @@
         in_specs=[in_vmem] * 3,
         out_specs=[anywhere, in_vmem, in_vmem],
         scratch_shapes=[pltpu.VMEM((BLK, BLK), f32), dma((8,))],
+        compiler_params=pltpu.CompilerParams(vmem_limit_bytes=8 << 20),
         name="finish",
-    )(sums, row, col)
+    )(*(pltpu.with_memory_space_constraint(v, pltpu.VMEM) for v in (sums, row, col)))
     return out, row.reshape(-1), col.reshape(-1)
 
 

time: 71.5 us -> 69.3 us (0.969)
  Pallas kernels: 70.7 us -> 68.5 us
    pallas_call x1, Pallas kernels: 2.85 us -> 1.62 us  [shards(): pl.pallas_call(finish, out_shape=(full, vec, vec), in_specs=[in_vmem] * 3...]
    pallas_call x1, Pallas kernels: 67.9 us -> 66.9 us  [shards(): pl.pallas_call(functools.partial(kernel, total_rows, total_cols), out_sha...]
where the time goes in v3:
time: 69.3 us; the launch traced here: 69.2 us
  Pallas kernels  68.5 us (99%)
    pallas_call x1, Pallas kernels, shards(): pl.pallas_call(functools.partial(kernel, total_rows, total_cols), out_sha...  66.9 us
    pallas_call x1, Pallas kernels, shards(): pl.pallas_call(finish, out_shape=(full, vec, vec), in_specs=[in_vmem] * 3...  1.62 us

profile of v3, /device:TPU:1, one launch (start us, length us, event | category | flops | bytes accessed | tf_op | source)
XLA Modules:
  0.0 69.2 jit_solution(7154884002400995529)
XLA Ops:
  0.6 66.9 %coupling_step.1 = (f32[512,512]{1,0:T(8,128)S(1)}, f32[4,128]{1,0:T(4,128)S(1)}, f32[4,128]{1,0:T(4,128)S(1)}) custom-call(bf16[512,512]{1,0:T(8,128)(2,1)} %coupling_hbm.1, bf16[50,512]{1,0:T(8,128)(2,1)} %src_hbm.1, bf16[50,512]{1,0:T(8,128)(2,1)} %tgt_hbm.1, f32[4,128]{1,0:T(4,128)} %bitcast.4, f32[4,128]{1,0:T(4,128)} %bitcast.5), custom_call_target="tpu_custom_call" | custom-call | tf_op jit(solution)/shard_map/coupling_step/pallas_call | solution.py:387
  67.6 1.6 %finish.1 = (f32[512,512]{1,0:T(8,128)}, f32[4,128]{1,0:T(4,128)}, f32[4,128]{1,0:T(4,128)}) custom-call(f32[512,512]{1,0:T(8,128)S(1)} %get-tuple-element.9.sum_ref, f32[4,128]{1,0:T(4,128)S(1)} %get-tuple-element.10.row_in, f32[4,128]{1,0:T(4,128)S(1)} %get-tuple-element.11.col_in), custom_call_target="tpu_custom_call" | custom-call | tf_op jit(solution)/shard_map/finish/pallas_call | solution.py:437

commit v4 on v3

--- a/solution.py
+++ b/solution.py
@@ -58,6 +58,16 @@
 
 def turn(pot):
     return jnp.concatenate([pot, jnp.zeros((120, 128), f32)], axis=0).T
+
+
+def join(top, total, v):
+    high = jnp.maximum(top, jnp.max(v, axis=0))
+    return high, total * jnp.exp2(top - high) + jnp.sum(jnp.exp2(v - high[None]), axis=0)
+
+
+def over_rows(tops, sums):
+    top = jnp.max(tops, axis=0, keepdims=True)
+    return top + jnp.log2(jnp.sum(sums * jnp.exp2(tops - top), axis=0, keepdims=True))
 
 
 def logsum_pass(table, pot, shift, out):
@@ -76,14 +86,9 @@
             for k in range(2):
                 j = 2 * pair + k
                 v = table[rows, j * 128 : (j + 1) * 128].reshape(16, 8, 128) + moved
-                top = jnp.maximum(tops[k], jnp.max(v, axis=0))
-                total = jnp.sum(jnp.exp2(v - top[None]), axis=0)
-                sums[k] = sums[k] * jnp.exp2(tops[k] - top) + total
-                tops[k] = top
+                tops[k], sums[k] = join(tops[k], sums[k], v)
         for k in range(2):
-            top = jnp.max(tops[k], axis=0, keepdims=True)
-            total = jnp.sum(sums[k] * jnp.exp2(tops[k] - top), axis=0, keepdims=True)
-            out[pl.ds(2 * pair + k, 1), :] = top + jnp.log2(total)
+            out[pl.ds(2 * pair + k, 1), :] = over_rows(tops[k], sums[k])
 
 
 def potentials(v, log_mass, log_count):
@@ -193,12 +198,17 @@
 
     rows56 = pl.ds(0, SENT)
 
-    def normed_of(packed_sum):
-        moment = packed_sum * (total_rows * total_cols) ** (-0.5)
-        square = jnp.sum(moment * moment, axis=1, keepdims=True)
-        square = jnp.sum(square, axis=0, keepdims=True) * (1.0 / (PCS * PCS))
-        scaled = moment / jnp.sqrt(square + tiny_eps) * (2.0 / (eps_reg * PCS) * LOG2E)
-        return jnp.concatenate([jnp.where(left, scaled, 0.0), jnp.where(left, 0.0, scaled)], axis=0)
+    def moment_of(packed_sum):
+        return packed_sum * (total_rows * total_cols) ** (-0.5)
+
+    def factor_of(packed_sum):
+        moment = moment_of(packed_sum)
+        square = jnp.sum(moment * moment, axis=0, keepdims=True)
+        square = jnp.sum(square, axis=1, keepdims=True) * (1.0 / (PCS * PCS))
+        return (2.0 / (eps_reg * PCS) * LOG2E) / jnp.sqrt(square + tiny_eps)
+
+    def packed_two(v):
+        return jnp.concatenate([jnp.where(left, v, 0.0), jnp.where(left, 0.0, v)], axis=0)
 
     log_rows, log_cols = math.log2(total_rows), math.log2(total_cols)
     partner = device(x, y, z, 1 - c)
@@ -212,8 +222,11 @@
         log_tgt = jnp.log2(tmass[0])
 
         settle(nrm, fin_recv.at[0])
-        weighted = fold3(jnp.dot(split3(normed_of(nrm[...])), tgt_two[...], preferred_element_type=f32))
-        sum_ref[...] = jnp.dot(src_t[pl.ds(0, BLK), :], stack4(weighted), preferred_element_type=f32)
+        two = packed_two(moment_of(nrm[...]))
+        raw = fold3(jnp.dot(split3(two), tgt_two[...], preferred_element_type=f32))
+        sum_ref[...] = jnp.dot(
+            src_t[pl.ds(0, BLK), :], stack4(raw * factor_of(nrm[...])), preferred_element_type=f32
+        )
 
         settle(pot, fin_recv.at[1])
         half = jnp.where(yh == 0, pot[pl.ds(0, 4), :], pot[pl.ds(4, 4), :])
@@ -276,26 +289,35 @@
             src_all[:, pl.ds(side * BLK, BLK)] = src_f[side].astype(bf16)
         log_src = jnp.log2(jnp.concatenate([smass[0], smass[1]], axis=0))
         log_tgt = jnp.log2(jnp.concatenate([tmass[0], tmass[1]], axis=0))
-        pot[...] = jnp.zeros((8, 128), f32)
 
         settle(m2_r.at[pl.ds(0, 7)], m_recv.at[2])
         total = jnp.sum(m2_r[...], axis=0)
         nrm[...] = total
         send(nrm, nrm, fin_send.at[0], fin_recv.at[0], partner)
 
-        two = normed_of(total)
-        turned = jnp.concatenate([two, jnp.zeros((PAD, 128), f32)], axis=0).T
+        turned = jnp.concatenate([packed_two(moment_of(total)), jnp.zeros((PAD, 128), f32)], axis=0).T
         back = turned[:PAD, :PAD] + turned[PAD:, :PAD]
-        weighted_t = stack4(fold3(jnp.dot(split3(back), src_all[...], preferred_element_type=f32)))
-        for n in range(8):
-            rows = pl.ds(n * 128, 128)
-            scores_t[rows, :] = jnp.dot(tgt_t[rows, :], weighted_t, preferred_element_type=f32)
+        factor = factor_of(total)
+        raw = fold3(jnp.dot(split3(back), src_all[...], preferred_element_type=f32))
+        weighted_t = stack4(raw * factor)
+        tops = [jnp.full((8, 128), -1e30, f32)] * 8
+        sums = [jnp.zeros((8, 128), f32)] * 8
+        for n in range(9):
+            if n < 8:
+                rows = pl.ds(n * 128, 128)
+                scores_t[rows, :] = jnp.dot(tgt_t[rows, :], weighted_t, preferred_element_type=f32)
+            if n:
+                rows = pl.ds((n - 1) * 128, 128)
+                for j in range(8):
+                    v = scores_t[rows, j * 128 : (j + 1) * 128].reshape(16, 8, 128)
+                    tops[j], sums[j] = join(tops[j], sums[j], v)
+        for j in range(8):
+            row_s[0, pl.ds(j, 1), :] = over_rows(tops[j], sums[j])
 
         row_slot = 4 * x + yl
         y_two = (y + 2 + 4 * (x % 2)) % 8
 
         def iteration(it, _):
-            logsum_pass(scores_t, pot[...], shift, row_s.at[it])
             for dx in (2, 1, 3, 0):
                 for ty in (y_two, (y + 1) % 8, (y + 7) % 8, y):
                     if dx or ty is not y:
@@ -305,7 +327,9 @@
 
             @pl.when(it == 0)
             def _():
-                weighted = stack4(fold3(jnp.dot(split3(two), tgt_all[...], preferred_element_type=f32)))
+                two = packed_two(moment_of(nrm[...]))
+                raw = fold3(jnp.dot(split3(two), tgt_all[...], preferred_element_type=f32))
+                weighted = stack4(raw * factor_of(nrm[...]))
                 for n in range(8):
                     rows = pl.ds(n * 128, 128)
                     scores[rows, :] = jnp.dot(src_t[rows, :], weighted, preferred_element_type=f32)
@@ -339,6 +363,11 @@
 
             settle(col_r.at[it, pl.ds(0, 7)], col_recv.at[it])
             pot[...] = potentials(col_r[it], log_tgt, log_rows)
+
+            @pl.when(it < last)
+            def _():
+                logsum_pass(scores_t, pot[...], shift, row_s.at[it + 1])
+
             return 0
 
         lax.fori_loop(0, ITERS, iteration, 0)

time: 69.3 us -> 68.6 us (0.990)
  Pallas kernels: 68.5 us -> 67.8 us
    pallas_call x1, Pallas kernels: 66.9 us -> 66.2 us  [shards(): pl.pallas_call(functools.partial(kernel, total_rows, total_cols), out_sha...]
where the time goes in v4:
time: 68.6 us; the launch traced here: 68.4 us
  Pallas kernels  67.8 us (99%)
    pallas_call x1, Pallas kernels, shards(): pl.pallas_call(functools.partial(kernel, total_rows, total_cols), out_sha...  66.2 us
    pallas_call x1, Pallas kernels, shards(): pl.pallas_call(finish, out_shape=(full, vec, vec), in_specs=[in_vmem] * 3...  1.62 us

profile of v4, /device:TPU:1, one launch (start us, length us, event | category | flops | bytes accessed | tf_op | source)
XLA Modules:
  0.0 68.4 jit_solution(6476368125765363375)
XLA Ops:
  0.6 66.2 %coupling_step.1 = (f32[512,512]{1,0:T(8,128)S(1)}, f32[4,128]{1,0:T(4,128)S(1)}, f32[4,128]{1,0:T(4,128)S(1)}) custom-call(bf16[512,512]{1,0:T(8,128)(2,1)} %coupling_hbm.1, bf16[50,512]{1,0:T(8,128)(2,1)} %src_hbm.1, bf16[50,512]{1,0:T(8,128)(2,1)} %tgt_hbm.1, f32[4,128]{1,0:T(4,128)} %bitcast.4, f32[4,128]{1,0:T(4,128)} %bitcast.5), custom_call_target="tpu_custom_call" | custom-call | tf_op jit(solution)/shard_map/coupling_step/pallas_call | solution.py:416
  66.8 1.6 %finish.1 = (f32[512,512]{1,0:T(8,128)}, f32[4,128]{1,0:T(4,128)}, f32[4,128]{1,0:T(4,128)}) custom-call(f32[512,512]{1,0:T(8,128)S(1)} %get-tuple-element.9.sum_ref, f32[4,128]{1,0:T(4,128)S(1)} %get-tuple-element.10.row_in, f32[4,128]{1,0:T(4,128)S(1)} %get-tuple-element.11.col_in), custom_call_target="tpu_custom_call" | custom-call | tf_op jit(solution)/shard_map/finish/pallas_call | solution.py:466

commit v5 on v4

--- a/solution.py
+++ b/solution.py
@@ -23,6 +23,21 @@
 MESH = pl.DeviceIdType.MESH
 f32, bf16 = jnp.float32, jnp.bfloat16
 FAR_X, FAR_8 = (2, 1, 3), (4, 3, 5, 2, 6, 1, 7)
+
+
+def hops(d):
+    return min(d[0], 4 - d[0]) + min(d[1], 8 - d[1])
+
+
+NEAR = sorted(
+    (
+        min(((dx, dy), ((dx + 2) % 4, dy + 4)), key=lambda d: (hops(d), (d[0] + d[1]) % 2, d))
+        for dx in range(4)
+        for dy in range(4)
+    ),
+    key=hops,
+    reverse=True,
+)[:-1]
 
 
 def coords():
@@ -118,10 +133,10 @@
     total_rows, total_cols,
     coupling_hbm, src_hbm, tgt_hbm, smass_hbm, tmass_hbm,
     sum_ref, row_ref, col_ref,
-    coupling, src_in, tgt_in, src_b, tgt_two, src_f, tgt_f, smass, tmass,
-    src_t, tgt_t, src_all, tgt_all, scores, scores_t, shift, pot,
+    coupling, src_in, tgt_in, src_b, tgt_two, src_f, tgt_f, tgt_k, smass, tmass, tmass_k,
+    src_t, tgt_t, src_all, tgt_all, tgt_own, scores, scores_t, shift, pot,
     m0_s, m0_r, m1_s, m1_r, m2_s, m2_r, nrm, row_s, row_r, col_s, col_r, fin_s,
-    load_sem, swap_send, swap_recv, m_send, m_recv, row_send, row_recv, col_send, col_recv, fin_send, fin_recv,
+    load_sem, swap_send, swap_recv, take_send, take_recv, m_send, m_recv, row_send, row_recv, col_send, col_recv, fin_send, fin_recv,
 ):
     x, y, z, c = coords()
     yh, yl = y // 4, y % 4
@@ -137,10 +152,8 @@
     for copy in loads:
         copy.start()
 
-    row_peers = [(dx, dy) for dx in (2, 1, 3, 0) for dy in (2, 6, 1, 7)]
-    ones = [device((x + dx) % 4, (y + dy) % 8, z, 1) for dx, dy in row_peers]
-    ones += [device((x + dx) % 4, y, z, 1) for dx in FAR_X]
-    ones += [device(x, (y + dy) % 8, z, 1) for dy in (4, 3, 5)]
+    plane = sorted({*NEAR, *((dx, 0) for dx in FAR_X), *((0, dy) for dy in FAR_8)}, key=hops, reverse=True)
+    ones = [device((x + dx) % 4, (y + dy) % 8, z, 1) for dx, dy in plane]
     ones += [device(x, y, (z + dz) % 8, 1) for dz in FAR_8]
     near = [device((x + dx) % 4, y, z, 0) for dx in (2, 1, 3, 0)]
 
@@ -189,6 +202,8 @@
         for dx in (2, 1, 3, 0):
             send(m0_s, m0_r.at[own0], m_send.at[0], m_recv.at[0], device((x + dx) % 4, y, z, 1))
 
+    for side in range(2):
+        tgt_k[side, pl.ds(SENT, 8), :] = jnp.zeros((8, BLK), f32)
     for ref, own, block in ((src_f, yh, src_b), (tgt_f, c, tgt_two)):
         for side in range(2):
             ref[side, pl.ds(SENT, 8), :] = jnp.zeros((8, BLK), f32)
@@ -258,8 +273,6 @@
 
     @pl.when(on_one)
     def _():
-        tgt_t[pl.ds(BLK, BLK), :] = thrice(tgt_f[1])
-
         settle(m0_r.at[pl.ds(0, 7)], m_recv.at[0])
         part = jnp.sum(m0_r[...], axis=0)
         m1_s[...] = part
@@ -269,11 +282,25 @@
 
         settle(tgt_f.at[0, rows56], swap_recv.at[0])
         settle(tmass.at[0], swap_recv.at[1])
-        tgt_t[pl.ds(0, BLK), :] = thrice(tgt_f[0])
-        near_b = tgt_f[0].astype(bf16)
-        tgt_all[pl.ds(0, PAD), pl.ds(0, BLK)] = near_b
-        tgt_all[pl.ds(PAD, PAD), pl.ds(0, BLK)] = near_b
-        tgt_all[:, pl.ds(BLK, BLK)] = tgt_two[...]
+
+        @pl.when(yh == 1)
+        def _():
+            target = device((x + 2) % 4, y, z, 1)
+            for core in range(2):
+                send(tgt_f.at[core, rows56], tgt_k.at[core, rows56], take_send.at[core], take_recv.at[core], target)
+            send(tmass, tmass_k, take_send.at[2], take_recv.at[2], target)
+
+        @pl.when(yh == 0)
+        def _():
+            for core in range(2):
+                tgt_k[core, rows56, :] = tgt_f[core, rows56, :]
+            tmass_k[...] = tmass[...]
+
+        for core in range(2):
+            lanes = pl.ds(core * BLK, BLK)
+            block = tgt_f[core].astype(bf16)
+            tgt_own[pl.ds(0, PAD), lanes] = block
+            tgt_own[pl.ds(PAD, PAD), lanes] = block
 
         settle(m1_r.at[pl.ds(0, 7)], m_recv.at[1])
         part = jnp.sum(m1_r[...], axis=0)
@@ -288,7 +315,21 @@
             src_t[pl.ds(side * BLK, BLK), :] = thrice(src_f[side])
             src_all[:, pl.ds(side * BLK, BLK)] = src_f[side].astype(bf16)
         log_src = jnp.log2(jnp.concatenate([smass[0], smass[1]], axis=0))
-        log_tgt = jnp.log2(jnp.concatenate([tmass[0], tmass[1]], axis=0))
+        log_own = jnp.log2(jnp.concatenate([tmass[0], tmass[1]], axis=0))
+
+        @pl.when(yh == 1)
+        def _():
+            for core in range(2):
+                settle(tgt_k.at[core, rows56], take_recv.at[core])
+            settle(tmass_k, take_recv.at[2])
+
+        log_tgt = jnp.log2(jnp.concatenate([tmass_k[0], tmass_k[1]], axis=0))
+        for core in range(2):
+            lanes = pl.ds(core * BLK, BLK)
+            tgt_t[lanes, :] = thrice(tgt_k[core])
+            block = tgt_k[core].astype(bf16)
+            tgt_all[pl.ds(0, PAD), lanes] = block
+            tgt_all[pl.ds(PAD, PAD), lanes] = block
 
         settle(m2_r.at[pl.ds(0, 7)], m_recv.at[2])
         total = jnp.sum(m2_r[...], axis=0)
@@ -314,25 +355,29 @@
         for j in range(8):
             row_s[0, pl.ds(j, 1), :] = over_rows(tops[j], sums[j])
 
-        row_slot = 4 * x + yl
-        y_two = (y + 2 + 4 * (x % 2)) % 8
+        row_slot = 4 * ((x + 2 * yh) % 4) + yl
+
+        def score(targets):
+            two = packed_two(moment_of(nrm[...]))
+            raw = fold3(jnp.dot(split3(two), targets[...], preferred_element_type=f32))
+            weighted = stack4(raw * factor_of(nrm[...]))
+            for n in range(8):
+                rows = pl.ds(n * 128, 128)
+                scores[rows, :] = jnp.dot(src_t[rows, :], weighted, preferred_element_type=f32)
 
         def iteration(it, _):
-            for dx in (2, 1, 3, 0):
-                for ty in (y_two, (y + 1) % 8, (y + 7) % 8, y):
-                    if dx or ty is not y:
-                        target = device((x + dx) % 4, ty, z, 1)
-                        send(row_s.at[it], row_r.at[it, row_slot], row_send.at[it], row_recv.at[it], target)
+            for dx, dy in NEAR:
+                target = device((x + 4 - dx) % 4, (y + 8 - dy) % 8, z, 1)
+                send(row_s.at[it], row_r.at[it, row_slot], row_send.at[it], row_recv.at[it], target)
             row_r[it, row_slot] = row_s[it]
 
             @pl.when(it == 0)
             def _():
-                two = packed_two(moment_of(nrm[...]))
-                raw = fold3(jnp.dot(split3(two), tgt_all[...], preferred_element_type=f32))
-                weighted = stack4(raw * factor_of(nrm[...]))
-                for n in range(8):
-                    rows = pl.ds(n * 128, 128)
-                    scores[rows, :] = jnp.dot(src_t[rows, :], weighted, preferred_element_type=f32)
+                score(tgt_all)
+
+            @pl.when(it == last)
+            def _():
+                score(tgt_own)
 
             settle(row_r.at[it, pl.ds(0, 15)], row_recv.at[it])
             row_pot = potentials(row_r[it], log_src, log_cols)
@@ -362,7 +407,7 @@
                         sum_ref[to, pl.ds(j * 128, 128)] = scores[rows, pl.ds(BLK + j * 128, 128)] + moved
 
             settle(col_r.at[it, pl.ds(0, 7)], col_recv.at[it])
-            pot[...] = potentials(col_r[it], log_tgt, log_rows)
+            pot[...] = potentials(col_r[it], jnp.where(it == last, log_own, log_tgt), log_rows)
 
             @pl.when(it < last)
             def _():
@@ -382,6 +427,12 @@
         for it in range(ITERS):
             settle(row_r.at[it, pl.ds(0, 15)], row_send.at[it])
             settle(col_r.at[it, pl.ds(0, 7)], col_send.at[it])
+
+    @pl.when(on_one & (yh == 1))
+    def _():
+        for core in range(2):
+            settle(tgt_f.at[core, rows56], take_send.at[core])
+        settle(tmass, take_send.at[2])
 
     @pl.when(on_one & edge)
     def _():
@@ -426,11 +477,14 @@
             pltpu.VMEM((2 * PAD, BLK), bf16),
             pltpu.VMEM((2, PAD, BLK), f32),
             pltpu.VMEM((2, PAD, BLK), f32),
+            pltpu.VMEM((2, PAD, BLK), f32),
+            pltpu.VMEM((2, 4, 128), f32),
             pltpu.VMEM((2, 4, 128), f32),
             pltpu.VMEM((2, 4, 128), f32),
             pltpu.VMEM((TWO, 4 * PAD), bf16),
             pltpu.VMEM((TWO, 4 * PAD), bf16),
             pltpu.VMEM((PAD, TWO), bf16),
+            pltpu.VMEM((2 * PAD, TWO), bf16),
             pltpu.VMEM((2 * PAD, TWO), bf16),
             pltpu.VMEM((TWO, TWO), f32),
             pltpu.VMEM((TWO, TWO), f32),
@@ -453,6 +507,8 @@
             dma((4,)),
             dma((3,)),
             dma((3,)),
+            dma((3,)),
+            dma((3,)),
             dma((ITERS,)),
             dma((ITERS,)),
             dma((ITERS,)),

time: 68.6 us -> 67.6 us (0.985)
  Pallas kernels: 67.8 us -> 66.8 us
    pallas_call x1, Pallas kernels: 66.2 us -> 65.2 us  [shards(): pl.pallas_call(functools.partial(kernel, total_rows, total_cols), out_sha...]
where the time goes in v5:
time: 67.6 us; the launch traced here: 67.5 us
  Pallas kernels  66.8 us (99%)
    pallas_call x1, Pallas kernels, shards(): pl.pallas_call(functools.partial(kernel, total_rows, total_cols), out_sha...  65.2 us
    pallas_call x1, Pallas kernels, shards(): pl.pallas_call(finish, out_shape=(full, vec, vec), in_specs=[in_vmem] * 3...  1.62 us

profile of v5, /device:TPU:1, one launch (start us, length us, event | category | flops | bytes accessed | tf_op | source)
XLA Modules:
  0.0 67.5 jit_solution(13794369141825124151)
XLA Ops:
  0.6 65.2 %coupling_step.1 = (f32[512,512]{1,0:T(8,128)S(1)}, f32[4,128]{1,0:T(4,128)S(1)}, f32[4,128]{1,0:T(4,128)S(1)}) custom-call(bf16[512,512]{1,0:T(8,128)(2,1)} %coupling_hbm.1, bf16[50,512]{1,0:T(8,128)(2,1)} %src_hbm.1, bf16[50,512]{1,0:T(8,128)(2,1)} %tgt_hbm.1, f32[4,128]{1,0:T(4,128)} %bitcast.4, f32[4,128]{1,0:T(4,128)} %bitcast.5), custom_call_target="tpu_custom_call" | custom-call | tf_op jit(solution)/shard_map/coupling_step/pallas_call | solution.py:467
  65.8 1.6 %finish.1 = (f32[512,512]{1,0:T(8,128)}, f32[4,128]{1,0:T(4,128)}, f32[4,128]{1,0:T(4,128)}) custom-call(f32[512,512]{1,0:T(8,128)S(1)} %get-tuple-element.9.sum_ref, f32[4,128]{1,0:T(4,128)S(1)} %get-tuple-element.10.row_in, f32[4,128]{1,0:T(4,128)S(1)} %get-tuple-element.11.col_in), custom_call_target="tpu_custom_call" | custom-call | tf_op jit(solution)/shard_map/finish/pallas_call | solution.py:522

commit v6 on v5

--- a/solution.py
+++ b/solution.py
@@ -18,6 +18,7 @@
 
 PAD = 64
 SENT = 56
+HELD = 26
 BLK = 512
 TWO = 2 * BLK
 MESH = pl.DeviceIdType.MESH
@@ -152,6 +153,10 @@
     for copy in loads:
         copy.start()
 
+    held = pl.ds(0, HELD)
+    for ref in (m0_r, m1_r, m2_r):
+        ref[:, pl.ds(HELD, 32 - HELD), :] = jnp.zeros((8, 32 - HELD, 128), f32)
+
     plane = sorted({*NEAR, *((dx, 0) for dx in FAR_X), *((0, dy) for dy in FAR_8)}, key=hops, reverse=True)
     ones = [device((x + dx) % 4, (y + dy) % 8, z, 1) for dx, dy in plane]
     ones += [device(x, y, (z + dz) % 8, 1) for dz in FAR_8]
@@ -166,12 +171,13 @@
         greet([device(x, y, (z + dz) % 8, 1) for dz in FAR_8])
         greet([device((x + dx) % 4, y, z, 1) for dx in (2, 1, 3, 0)])
 
-    src_b[pl.ds(48, 16), :] = jnp.zeros((16, BLK), bf16)
+    src_b[...] = jnp.zeros((PAD, BLK), bf16)
     tgt_two[pl.ds(48, 16), :] = jnp.zeros((16, BLK), bf16)
     tgt_two[pl.ds(112, 16), :] = jnp.zeros((16, BLK), bf16)
     for copy in loads[:2]:
         copy.wait()
-    src_b[pl.ds(0, PCS), :] = src_in[...]
+    src_b[pl.ds(0, HELD), :] = src_in[pl.ds(0, HELD), :]
+    src_b[pl.ds(32, PCS - HELD), :] = src_in[pl.ds(HELD, PCS - HELD), :]
     tgt_two[pl.ds(0, PCS), :] = tgt_in[...]
     tgt_two[pl.ds(PAD, PCS), :] = tgt_in[...]
     loads[2].wait()
@@ -192,15 +198,15 @@
     @pl.when(on_one)
     def _():
         pl.semaphore_wait(barrier, len(ones) + 7 + 4)
-        m0_r[own0] = packed
+        m0_r[own0, held] = packed[:HELD]
         for dx in FAR_X:
-            send(m0_s, m0_r.at[own0], m_send.at[0], m_recv.at[0], device((x + dx) % 4, y, z, 1))
+            send(m0_s.at[held], m0_r.at[own0, held], m_send.at[0], m_recv.at[0], device((x + dx) % 4, y, z, 1))
 
     @pl.when(on_zero)
     def _():
         pl.semaphore_wait(barrier, 4)
         for dx in (2, 1, 3, 0):
-            send(m0_s, m0_r.at[own0], m_send.at[0], m_recv.at[0], device((x + dx) % 4, y, z, 1))
+            send(m0_s.at[held], m0_r.at[own0, held], m_send.at[0], m_recv.at[0], device((x + dx) % 4, y, z, 1))
 
     for side in range(2):
         tgt_k[side, pl.ds(SENT, 8), :] = jnp.zeros((8, BLK), f32)
@@ -257,7 +263,7 @@
         settle(col_r.at[last], col_recv.at[last])
         col_ref[...] = potentials(col_r[last][:, :4, :], log_tgt, log_rows)
 
-        settle(m0_r.at[pl.ds(0, 4)], m_send.at[0])
+        settle(m0_r.at[pl.ds(0, 4), held], m_send.at[0])
         settle(tgt_f.at[0, rows56], swap_send.at[0])
         settle(tmass.at[0], swap_send.at[1])
 
@@ -273,12 +279,12 @@
 
     @pl.when(on_one)
     def _():
-        settle(m0_r.at[pl.ds(0, 7)], m_recv.at[0])
+        settle(m0_r.at[pl.ds(0, 7), held], m_recv.at[0])
         part = jnp.sum(m0_r[...], axis=0)
         m1_s[...] = part
         for dy in FAR_8:
-            send(m1_s, m1_r.at[y], m_send.at[1], m_recv.at[1], device(x, (y + dy) % 8, z, 1))
-        m1_r[y] = part
+            send(m1_s.at[held], m1_r.at[y, held], m_send.at[1], m_recv.at[1], device(x, (y + dy) % 8, z, 1))
+        m1_r[y, held] = part[:HELD]
 
         settle(tgt_f.at[0, rows56], swap_recv.at[0])
         settle(tmass.at[0], swap_recv.at[1])
@@ -302,12 +308,12 @@
             tgt_own[pl.ds(0, PAD), lanes] = block
             tgt_own[pl.ds(PAD, PAD), lanes] = block
 
-        settle(m1_r.at[pl.ds(0, 7)], m_recv.at[1])
+        settle(m1_r.at[pl.ds(0, 7), held], m_recv.at[1])
         part = jnp.sum(m1_r[...], axis=0)
         m2_s[...] = part
         for dz in FAR_8:
-            send(m2_s, m2_r.at[z], m_send.at[2], m_recv.at[2], device(x, y, (z + dz) % 8, 1))
-        m2_r[z] = part
+            send(m2_s.at[held], m2_r.at[z, held], m_send.at[2], m_recv.at[2], device(x, y, (z + dz) % 8, 1))
+        m2_r[z, held] = part[:HELD]
 
         settle(src_f.at[0, rows56], swap_recv.at[2])
         settle(smass.at[0], swap_recv.at[3])
@@ -331,7 +337,7 @@
             tgt_all[pl.ds(0, PAD), lanes] = block
             tgt_all[pl.ds(PAD, PAD), lanes] = block
 
-        settle(m2_r.at[pl.ds(0, 7)], m_recv.at[2])
+        settle(m2_r.at[pl.ds(0, 7), held], m_recv.at[2])
         total = jnp.sum(m2_r[...], axis=0)
         nrm[...] = total
         send(nrm, nrm, fin_send.at[0], fin_recv.at[0], partner)
@@ -418,9 +424,9 @@
         lax.fori_loop(0, ITERS, iteration, 0)
         col_ref[...] = pot[pl.ds(4, 4), :]
 
-        settle(m0_r.at[pl.ds(0, 3)], m_send.at[0])
-        settle(m1_r.at[pl.ds(0, 7)], m_send.at[1])
-        settle(m2_r.at[pl.ds(0, 7)], m_send.at[2])
+        settle(m0_r.at[pl.ds(0, 3), held], m_send.at[0])
+        settle(m1_r.at[pl.ds(0, 7), held], m_send.at[1])
+        settle(m2_r.at[pl.ds(0, 7), held], m_send.at[2])
         settle(nrm, fin_send.at[0])
         settle(fin_s, fin_send.at[1])
         settle(col_r.at[last], fin_send.at[2])

time: 67.6 us -> 67.2 us (level)
  no operation moved by 1% of the time
where the time goes in v6:
time: 67.2 us; the launch traced here: 67.1 us
  Pallas kernels  66.4 us (99%)
    pallas_call x1, Pallas kernels, shards(): pl.pallas_call(functools.partial(kernel, total_rows, total_cols), out_sha...  64.8 us
    pallas_call x1, Pallas kernels, shards(): pl.pallas_call(finish, out_shape=(full, vec, vec), in_specs=[in_vmem] * 3...  1.62 us

profile of v6, /device:TPU:1, one launch (start us, length us, event | category | flops | bytes accessed | tf_op | source)
XLA Modules:
  0.0 67.1 jit_solution(9978361052638362566)
XLA Ops:
  0.6 64.8 %coupling_step.1 = (f32[512,512]{1,0:T(8,128)S(1)}, f32[4,128]{1,0:T(4,128)S(1)}, f32[4,128]{1,0:T(4,128)S(1)}) custom-call(bf16[512,512]{1,0:T(8,128)(2,1)} %coupling_hbm.1, bf16[50,512]{1,0:T(8,128)(2,1)} %src_hbm.1, bf16[50,512]{1,0:T(8,128)(2,1)} %tgt_hbm.1, f32[4,128]{1,0:T(4,128)} %bitcast.4, f32[4,128]{1,0:T(4,128)} %bitcast.5), custom_call_target="tpu_custom_call" | custom-call | tf_op jit(solution)/shard_map/coupling_step/pallas_call | solution.py:473
  65.4 1.6 %finish.1 = (f32[512,512]{1,0:T(8,128)}, f32[4,128]{1,0:T(4,128)}, f32[4,128]{1,0:T(4,128)}) custom-call(f32[512,512]{1,0:T(8,128)S(1)} %get-tuple-element.9.sum_ref, f32[4,128]{1,0:T(4,128)S(1)} %get-tuple-element.10.row_in, f32[4,128]{1,0:T(4,128)S(1)} %get-tuple-element.11.col_in), custom_call_target="tpu_custom_call" | custom-call | tf_op jit(solution)/shard_map/finish/pallas_call | solution.py:528
